TPU v7x, 256 devices: a whole 4x4x8 slice. The times are simulated.
256 devices in a mesh: dp: 8 (over z_lo, y), seq: 32 (over x, z_hi, core).
Axes of the slice: x: 4, y: 4, z: 8 (z_hi: 4, z_lo: 2; z = z_hi * 2 + z_lo), core: 2. Of those that a mesh axis runs over, the one named last changes fastest.
Arguments:
- tokens: bfloat16 [8, 8192, 4096], P('dp', 'seq'), may hold values from -6 to 6
- queries: bfloat16 [8, 8192, 128], P('dp', 'seq'), may hold values from -6 to 6
- key_vectors: bfloat16 [8, 8192, 128], P('dp', 'seq'), may hold values from -6 to 6
- doc_position: int32 [8, 8192], P('dp', 'seq'), may hold values from 0 to 8191, as said below
- value_scores: float32 [8, 8192, 4], P('dp', 'seq'), may hold values from 0.1 to 1
- value_experts: int32 [8, 8192, 2], P('dp', 'seq'), may hold values from 0 to 3, all different within a row
- output_scores: float32 [8, 8192, 4], P('dp', 'seq'), may hold values from 0.1 to 1
- output_experts: int32 [8, 8192, 2], P('dp', 'seq'), may hold values from 0 to 3, all different within a row
- value_panels: bfloat16 [4096, 512], P('seq'), may hold values from -0.09375 to 0.09375
- output_panels: bfloat16 [4096, 512], P('seq'), may hold values from -3 to 3
- cotangent: bfloat16 [8, 8192, 4096], P('dp', 'seq'), may hold values from -0.625 to 0.625
Outputs:
- layer_output: bfloat16 [8, 8192, 4096], P('dp', 'seq')
- grad_tokens: bfloat16 [8, 8192, 4096], P('dp', 'seq')
- grad_queries: bfloat16 [8, 8192, 128], P('dp', 'seq')
- grad_keys: bfloat16 [8, 8192, 128], P('dp', 'seq')
- grad_value: float32 [4096, 512], P('seq')
- grad_output: float32 [4096, 512], P('seq')
Inputs may be any that keep to these rules, and one draw needn't show every extreme that they name: doc_position[b, i] is i minus the first position of the document that holds position i; position 0 starts a document in every sequence; sequence 0 is one document; every other sequence holds one to four documents.
All inputs are finite; a program needn't handle non-finite values.
Results may differ from a plain program's by a relative error of at most 0.035.
Values may be sent and summed in bfloat16 or wider, within the bound.
No kernel may reach another device: no remote copies, remote signals or barrier semaphores. Data moves between devices by JAX's collectives and lax.ppermute only.
A program may use at most 128 MiB of HBM per device.

v0:
```python
import jax
import jax.numpy as jnp
from jax import lax
from jax.sharding import PartitionSpec as P


def expert_gates(scores, chosen, experts):
    chosen_hit = chosen[:, :, None] == lax.iota(jnp.int32, experts)[None, None, :]
    return jnp.where(jnp.any(chosen_hit, axis=1), scores, jnp.float32(0.0))


def contract_last(left, right):
    return lax.dot_general(
        left, right, (((1,), (1,)), ((), ())), preferred_element_type=jnp.float32
    )


def contract_first(left, right):
    return lax.dot_general(
        left, right, (((0,), (0,)), ((), ())), preferred_element_type=jnp.float32
    )


def body(
    tokens,
    queries,
    key_vectors,
    doc_position,
    value_scores,
    value_experts,
    output_scores,
    output_experts,
    value_panels,
    output_panels,
    cotangent,
):
    tok_block = tokens[0]
    query_block = queries[0]
    own_keys = key_vectors[0]
    positions = doc_position[0]
    grad_rows = cotangent[0]
    tok_rows = tok_block.shape[0]
    head_size = query_block.shape[1]
    experts = value_scores.shape[2]
    panel_width = value_panels.shape[1]
    value_gate = expert_gates(value_scores[0], value_experts[0], experts)
    output_gate = expert_gates(output_scores[0], output_experts[0], experts)
    value_full, output_full = (
        lax.all_gather(value_panels, "seq", axis=0, tiled=True),
        lax.all_gather(output_panels, "seq", axis=0, tiled=True),
    )
    projection = jnp.dot(tok_block, value_full, preferred_element_type=jnp.float32)
    value_vec = jnp.sum(
        projection.reshape(tok_rows, experts, head_size) * value_gate[:, :, None], axis=1
    ).astype(jnp.bfloat16)
    keys_all, values_all = (
        lax.all_gather(own_keys, "seq", axis=0, tiled=True),
        lax.all_gather(value_vec, "seq", axis=0, tiled=True),
    )
    length = keys_all.shape[0]
    score_scale = head_size ** (-0.5)
    query_index = lax.axis_index("seq") * tok_rows + lax.iota(jnp.int32, tok_rows)
    key_index = lax.iota(jnp.int32, length)
    visible = (key_index[None, :] <= query_index[:, None]) & (
        query_index[:, None] - key_index[None, :] <= positions[:, None]
    )
    masked = jnp.where(visible, contract_last(query_block, keys_all) * score_scale, -jnp.inf)
    row_max = jnp.max(masked, axis=1)
    log_total = row_max + jnp.log(jnp.sum(jnp.exp(masked - row_max[:, None]), axis=1))
    attn_prob = jnp.exp(masked - log_total[:, None])
    prob_low = attn_prob.astype(jnp.bfloat16)
    attended = jnp.dot(prob_low, values_all, preferred_element_type=jnp.float32).astype(
        jnp.bfloat16
    )
    expanded = (
        (output_gate[:, :, None] * attended.astype(jnp.float32)[:, None, :])
        .reshape(tok_rows, panel_width)
        .astype(jnp.bfloat16)
    )
    layer_output = contract_last(expanded, output_full).astype(jnp.bfloat16)
    pulled = jnp.dot(grad_rows, output_full, preferred_element_type=jnp.float32)
    dattended = jnp.sum(
        pulled.reshape(tok_rows, experts, head_size) * output_gate[:, :, None], axis=1
    ).astype(jnp.bfloat16)
    row_delta = jnp.sum(dattended.astype(jnp.float32) * attended.astype(jnp.float32), axis=1)
    dweights = contract_last(dattended, values_all)
    dscores = (attn_prob * (dweights - row_delta[:, None])).astype(jnp.bfloat16)
    grad_queries = (
        jnp.dot(dscores, keys_all, preferred_element_type=jnp.float32) * score_scale
    ).astype(jnp.bfloat16)
    key_term = contract_first(dscores, query_block) * score_scale
    value_term = contract_first(prob_low, dattended)
    dkey_sum, dvalue_sum = (
        lax.psum_scatter(
            key_term.astype(jnp.bfloat16), "seq", scatter_dimension=0, tiled=True
        ).astype(jnp.float32),
        lax.psum_scatter(
            value_term.astype(jnp.bfloat16), "seq", scatter_dimension=0, tiled=True
        ).astype(jnp.float32),
    )
    grad_keys = dkey_sum.astype(jnp.bfloat16)
    dvalue = dvalue_sum.astype(jnp.bfloat16)
    value_grad = (
        (value_gate[:, :, None] * dvalue.astype(jnp.float32)[:, None, :])
        .reshape(tok_rows, panel_width)
        .astype(jnp.bfloat16)
    )
    grad_tokens = contract_last(value_grad, value_full).astype(jnp.bfloat16)
    term_value = contract_first(tok_block, value_grad)
    term_output = contract_first(grad_rows, expanded)
    owned = lax.psum_scatter(
        jnp.concatenate([term_value, term_output], axis=1).astype(jnp.bfloat16),
        "seq",
        scatter_dimension=0,
        tiled=True,
    )
    summed = lax.psum(owned, "dp").astype(jnp.float32)
    return (
        layer_output[None],
        grad_tokens[None],
        grad_queries[None],
        grad_keys[None],
        summed[:, :panel_width],
        summed[:, panel_width:],
    )


def solution(mesh):
    in_specs = (
        P("dp", "seq", None),
        P("dp", "seq", None),
        P("dp", "seq", None),
        P("dp", "seq"),
        P("dp", "seq", None),
        P("dp", "seq", None),
        P("dp", "seq", None),
        P("dp", "seq", None),
        P("seq", None),
        P("seq", None),
        P("dp", "seq", None),
    )
    out_specs = (
        P("dp", "seq", None),
        P("dp", "seq", None),
        P("dp", "seq", None),
        P("dp", "seq", None),
        P("seq", None),
        P("seq", None),
    )
    return jax.shard_map(body, mesh=mesh, in_specs=in_specs, out_specs=out_specs, check_vma=False)
```

profile of v0, /device:TPU:8, one launch (start us, length us, event | category | flops | bytes accessed | tf_op | source)
XLA Modules:
  0.0 667.2 jit_solution(10940611194924719588)
XLA Ops:
  10.9 57.3 %all-gather.12.cloned.1.call-done = bf16[1,8192,128]{2,1,0:T(8,128)(2,1)} async-done(((bf16[1,256,128]{2,1,0:T(8,128)(2,1)}), bf16[1,8192,128]{2,1,0:T(8,128)(2,1)}) %all-gather.12.cloned.1.call-update) | async-done | bytes 2097168 | tf_op jit(solution)/shard_map/all_gather | solution.py:57
  68.2 4.6 fusion.50
  74.1 1.9 copy-done.2
  76.0 52.1 %all-gather.10.cloned.1.call-done = bf16[4096,512]{1,0:T(8,128)(2,1)} async-done(((bf16[128,512]{1,0:T(8,128)(2,1)}), bf16[4096,512]{1,0:T(8,128)(2,1)}) %all-gather.10.cloned.1.call-update) | async-done | bytes 4194320 | tf_op jit(solution)/shard_map/all_gather | solution.py:50
  128.1 6.4 copy.46
  134.5 4.1 fusion.25
  138.7 6.7 convolution_convert_fusion
  145.5 43.1 %all-gather.6.cloned.1.call-done = bf16[4096,512]{1,0:T(8,128)(2,1)} async-done(((bf16[128,512]{1,0:T(8,128)(2,1)}), bf16[4096,512]{1,0:T(8,128)(2,1)}) %all-gather.6.cloned.1.call-update) | async-done | bytes 4194320 | tf_op jit(solution)/shard_map/all_gather | solution.py:49
  188.6 6.4 copy.43
  195.0 4.1 fusion.28
  199.4 82.5 %reduce-scatter.6.cloned.1.call-done = bf16[256,128]{1,0:T(8,128)(2,1)} async-done(((bf16[8192,128]{1,0:T(8,128)(2,1)}), bf16[256,128]{1,0:T(8,128)(2,1)}) %reduce-scatter.6.cloned.1.call-update) | async-done | bytes 65552 | tf_op jit(solution)/shard_map/reduce_scatter | solution.py:97
  283.1 3.2 fusion.6
  286.3 50.8 %all-gather.8.cloned.1.call-done = bf16[8192,128]{1,0:T(8,128)(2,1)} async-done(((bf16[256,128]{1,0:T(8,128)(2,1)}), bf16[8192,128]{1,0:T(8,128)(2,1)}) %all-gather.8.cloned.1.call-update) | async-done | bytes 2097168 | tf_op jit(solution)/shard_map/all_gather | solution.py:58
  337.1 5.7 multiply_reduce_fusion
  343.3 3.2 fusion.7
  346.5 7.8 %pad_maximum_fusion = bf16[4096,1024]{0,1:T(8,128)(2,1)} fusion(bf16[4096,512]{0,1:T(8,128)(2,1)} %fusion.7, bf16[4096,512]{0,1:T(8,128)(2,1)} %fusion.6), kind=kLoop, calls=%fused_computation.8 | loop fusion | flops 16777216 | bytes 16777216 | tf_op jit(solution)/shard_map/concatenate | solution.py:112
  354.3 12.0 %copy.51 = bf16[4096,1024]{1,0:T(8,128)(2,1)} copy(bf16[4096,1024]{0,1:T(8,128)(2,1)} %pad_maximum_fusion) | data formatting | bytes 16777216
  367.9 6.1 fusion.2
  374.0 111.0 %reduce-scatter.10.cloned.1.call-done = bf16[128,1024]{1,0:T(8,128)(2,1)} async-done(((bf16[4096,1024]{1,0:T(8,128)(2,1)}), bf16[128,1024]{1,0:T(8,128)(2,1)}) %reduce-scatter.10.cloned.1.call-update) | async-done | bytes 262160
  487.0 4.8 fusion.3
  491.9 5.0 fusion.9
  496.9 2.6 fusion.8
  502.4 60.6 %all-reduce.2.cloned.1.call-done = bf16[128,1024]{0,1:T(8,128)(2,1)} async-done(((bf16[128,1024]{0,1:T(8,128)(2,1)}), bf16[128,1024]{0,1:T(8,128)(2,1)}) %all-reduce.2.cloned.1.call-update) | async-done | bytes 262160 | tf_op jit(solution)/shard_map/psum | solution.py:117
  565.7 94.6 %reduce-scatter.8.cloned.1.call-done = bf16[256,128]{1,0:T(8,128)(2,1)} async-done(((bf16[8192,128]{1,0:T(8,128)(2,1)}), bf16[256,128]{1,0:T(8,128)(2,1)}) %reduce-scatter.8.cloned.1.call-update) | async-done | bytes 65552 | tf_op jit(solution)/shard_map/reduce_scatter | solution.py:94
  (56 shorter events, 16.3 us)
Async XLA Ops:
  7.2 187.8 %copy-start = (bf16[1,256,4096]{2,1,0:T(8,128)(2,1)S(1)}, bf16[1,256,4096]{2,1,0:T(8,128)(2,1)}, u32[]{:S(2)}) copy-start(bf16[1,256,4096]{2,1,0:T(8,128)(2,1)} %param.11) | copy-start | bytes 6291460
  7.2 61.0 %all-gather.12.cloned.1.call-start = ((), (), s32[]{:S(2)}) async-start(), calls=%async_computation.9 | async-start | bytes 2162688 | tf_op jit(solution)/shard_map/all_gather | solution.py:57
  7.9 120.2 %all-gather.10.cloned.1.call-start = ((), (), s32[]{:S(2)}) async-start(), calls=%async_computation.5 | async-start | bytes 4325376 | tf_op jit(solution)/shard_map/all_gather | solution.py:50
  8.7 179.9 %all-gather.6.cloned.1.call-start = ((), (), s32[]{:S(2)}) async-start(), calls=%async_computation.3 | async-start | bytes 4325376 | tf_op jit(solution)/shard_map/all_gather | solution.py:49
  9.4 272.5 %reduce-scatter.6.cloned.1.call-start = ((), (), s32[]{:S(2)}) async-start(), calls=%async_computation.6 | async-start | bytes 2162688 | tf_op jit(solution)/shard_map/reduce_scatter | solution.py:97
  72.8 3.2 copy-start.2
  138.7 6.8 %copy-start.10 = (s32[1,256,2]{1,2,0:T(2,128)S(1)}, s32[1,256,2]{1,2,0:T(2,128)}, u32[]{:S(2)}) copy-start(s32[1,256,2]{1,2,0:T(2,128)} %param.16) | copy-start | bytes 6148
  138.7 6.8 %copy-start.9 = (f32[1,256,4]{1,2,0:T(4,128)S(1)}, f32[1,256,4]{1,2,0:T(4,128)}, u32[]{:S(2)}) copy-start(f32[1,256,4]{1,2,0:T(4,128)} %param.15) | copy-start | bytes 12292
  145.4 191.7 %all-gather.8.cloned.1.call-start = ((), (), s32[]{:S(2)}) async-start(), calls=%async_computation.4 | async-start | bytes 2162688 | tf_op jit(solution)/shard_map/all_gather | solution.py:58
  199.1 285.8 %reduce-scatter.10.cloned.1.call-start = ((), (), s32[]{:S(2)}) async-start(), calls=%async_computation.10 | async-start | bytes 8650752
  286.3 57.0 %copy-start.6 = (bf16[1,256,4096]{2,1,0:T(8,128)(2,1)S(1)}, bf16[1,256,4096]{2,1,0:T(8,128)(2,1)}, u32[]{:S(2)}) copy-start(bf16[1,256,4096]{2,1,0:T(8,128)(2,1)} %param.21) | copy-start | bytes 6291460
  366.3 1.6 copy-start.5
  366.3 196.7 %all-reduce.2.cloned.1.call-start = ((), (), s32[]{:S(2)}) async-start(), calls=%async_computation.8 | async-start | bytes 524288 | tf_op jit(solution)/shard_map/psum | solution.py:117
  367.9 119.1 %copy-start.8 = (bf16[1,256,128]{2,1,0:T(8,128)(2,1)S(1)}, bf16[1,256,128]{2,1,0:T(8,128)(2,1)}, u32[]{:S(2)}) copy-start(bf16[1,256,128]{2,1,0:T(8,128)(2,1)} %param.12) | copy-start | bytes 196612
  486.7 173.6 %reduce-scatter.8.cloned.1.call-start = ((), (), s32[]{:S(2)}) async-start(), calls=%async_computation.7 | async-start | bytes 2162688 | tf_op jit(solution)/shard_map/reduce_scatter | solution.py:94
  491.9 5.0 copy-start.4
  496.9 2.6 copy-start.3
  496.9 3.6 copy-start.7
  496.9 163.5 %copy-start.1 = (bf16[1,256,4096]{2,1,0:T(8,128)(2,1)S(1)}, bf16[1,256,4096]{2,1,0:T(8,128)(2,1)}, u32[]{:S(2)}) copy-start(bf16[1,256,4096]{2,1,0:T(8,128)(2,1)} %param.11) | copy-start | bytes 6291460
Sparse Core Ops, SparseCore 0:
  10.6 57.5 all-gather.11
  70.7 57.3 all-gather.9
  130.6 57.8 all-gather.5
  192.8 88.9 reduce-scatter.5
  284.8 52.2 all-gather.7
  366.5 118.4 reduce-scatter.9
  488.3 74.6 all-reduce.1
  567.4 92.8 reduce-scatter.7
where the time goes:
time: 668 us; the launch traced here: 667 us
  waiting for transfers between devices  554 us (83%)
  matrix products  52 us (8%)
  local copies, waits for them, and re-layouts  34.1 us (5%)
  between operations  14.3 us (2%)
  other arithmetic  11.8 us (2%)
    unnamed x9, waiting for transfers between devices  113 us
    reduce_scatter x1, waiting for transfers between devices, body(): lax.psum_scatter(key_term.astype(jnp.bfloat16), 'seq', scatter_dimension=...  94.6 us
    reduce_scatter x1, waiting for transfers between devices, body(): lax.psum_scatter(value_term.astype(jnp.bfloat16), 'seq', scatter_dimensio...  82.5 us
    psum x1, waiting for transfers between devices, body(): summed = lax.psum(owned, 'dp').astype(jnp.float32)  60.6 us
    all_gather x1, waiting for transfers between devices, body(): lax.all_gather(own_keys, 'seq', axis=0, tiled=True)  57.3 us
    all_gather x1, waiting for transfers between devices, body(): lax.all_gather(output_panels, 'seq', axis=0, tiled=True)  52.1 us
    all_gather x1, waiting for transfers between devices, body(): lax.all_gather(value_vec, 'seq', axis=0, tiled=True)  50.8 us
    all_gather x1, waiting for transfers between devices, body(): lax.all_gather(value_panels, 'seq', axis=0, tiled=True)  43.1 us
  transfers between devices with their start and end apart: 8, of which 8 were waited for; matrix products, arithmetic and copies ran while one was open for 9% of the time, Pallas kernels for 0%

commit v1 on v0

--- a/solution.py
+++ b/solution.py
@@ -114,7 +114,7 @@
         scatter_dimension=0,
         tiled=True,
     )
-    summed = lax.psum(owned, "dp").astype(jnp.float32)
+    summed = jnp.sum(lax.all_gather(owned, "dp"), axis=0).astype(jnp.float32)
     return (
         layer_output[None],
         grad_tokens[None],

time: 668 us -> 637 us (0.954)
  waiting for transfers between devices: 554 us -> 523 us
    psum x1 -> x0, waiting for transfers between devices: 60.6 us -> none  [body(): summed = lax.psum(owned, 'dp').astype(jnp.float32)]
    all_gather x0 -> x1, waiting for transfers between devices: none -> 25.7 us  [body(): summed = jnp.sum(lax.all_gather(owned, 'dp'), axis=0).astype(jnp.float32)]
    unnamed x9, waiting for transfers between devices: 113 us -> 120 us
    unnamed x26 -> x29, local copies, waits for them, and re-layouts: 19.9 us -> 22.7 us
  transfers between devices with their start and end apart: 8 -> 8, of which waited for: 8 -> 8; matrix products, arithmetic and copies ran while one was open for 9% -> 10% of each run, Pallas kernels for 0% -> 0%
where the time goes in v1:
time: 637 us; the launch traced here: 636 us
  waiting for transfers between devices  523 us (82%)
  matrix products  48.6 us (8%)
  local copies, waits for them, and re-layouts  36 us (6%)
  between operations  14.3 us (2%)
  other arithmetic  13.4 us (2%)
    unnamed x9, waiting for transfers between devices  120 us
    reduce_scatter x1, waiting for transfers between devices, body(): lax.psum_scatter(key_term.astype(jnp.bfloat16), 'seq', scatter_dimension=...  91.2 us
    reduce_scatter x1, waiting for transfers between devices, body(): lax.psum_scatter(value_term.astype(jnp.bfloat16), 'seq', scatter_dimensio...  82.5 us
    all_gather x1, waiting for transfers between devices, body(): lax.all_gather(own_keys, 'seq', axis=0, tiled=True)  57.3 us
    all_gather x1, waiting for transfers between devices, body(): lax.all_gather(output_panels, 'seq', axis=0, tiled=True)  52.1 us
    all_gather x1, waiting for transfers between devices, body(): lax.all_gather(value_vec, 'seq', axis=0, tiled=True)  50.8 us
    all_gather x1, waiting for transfers between devices, body(): lax.all_gather(value_panels, 'seq', axis=0, tiled=True)  43.1 us
    all_gather x1, waiting for transfers between devices, body(): summed = jnp.sum(lax.all_gather(owned, 'dp'), axis=0).astype(jnp.float32)  25.7 us
  transfers between devices with their start and end apart: 8, of which 8 were waited for; matrix products, arithmetic and copies ran while one was open for 10% of the time, Pallas kernels for 0%

profile of v1, /device:TPU:8, one launch (start us, length us, event | category | flops | bytes accessed | tf_op | source)
XLA Modules:
  0.0 636.2 jit_solution(8925066934997801380)
XLA Ops:
  10.9 57.3 %all-gather.14.cloned.1.call-done = bf16[1,8192,128]{2,1,0:T(8,128)(2,1)} async-done(((bf16[1,256,128]{2,1,0:T(8,128)(2,1)}), bf16[1,8192,128]{2,1,0:T(8,128)(2,1)}) %all-gather.14.cloned.1.call-update) | async-done | bytes 2097168 | tf_op jit(solution)/shard_map/all_gather | solution.py:57
  68.2 4.6 fusion.50
  76.0 52.1 %all-gather.12.cloned.1.call-done = bf16[4096,512]{1,0:T(8,128)(2,1)} async-done(((bf16[128,512]{1,0:T(8,128)(2,1)}), bf16[4096,512]{1,0:T(8,128)(2,1)}) %all-gather.12.cloned.1.call-update) | async-done | bytes 4194320 | tf_op jit(solution)/shard_map/all_gather | solution.py:50
  128.1 6.4 %copy.42 = bf16[512,4096]{1,0:T(8,128)(2,1)} copy(bf16[512,4096]{0,1:T(8,128)(2,1)} %bitcast.84) | data formatting | bytes 8388608 | tf_op jit(solution)/shard_map/dot_general | solution.py:81
  134.5 4.1 fusion.25
  138.7 6.7 %convolution_convert_fusion = bf16[8192,128]{1,0:T(8,128)(2,1)} fusion(bf16[256,128]{0,1:T(8,128)(2,1)S(1)} %copy.43, f32[256,8192]{1,0:T(8,128)} %copy-done.2, f32[256]{0:T(256)S(1)} %log_add_fusion), kind=kOutput, calls=%fused_computation.7 | convolution fusion | flops 542113792 | bytes 10552320 | tf_op jit(solution)/shard_map/dot_general | solution.py:19
  145.5 43.1 %all-gather.8.cloned.1.call-done = bf16[4096,512]{1,0:T(8,128)(2,1)} async-done(((bf16[128,512]{1,0:T(8,128)(2,1)}), bf16[4096,512]{1,0:T(8,128)(2,1)}) %all-gather.8.cloned.1.call-update) | async-done | bytes 4194320 | tf_op jit(solution)/shard_map/all_gather | solution.py:49
  188.6 6.4 %copy.39 = bf16[512,4096]{1,0:T(8,128)(2,1)} copy(bf16[512,4096]{0,1:T(8,128)(2,1)} %bitcast.85) | data formatting | bytes 8388608 | tf_op jit(solution)/shard_map/dot_general | solution.py:52
  195.0 4.1 fusion.28
  199.4 82.5 %reduce-scatter.6.cloned.1.call-done = bf16[256,128]{1,0:T(8,128)(2,1)} async-done(((bf16[8192,128]{1,0:T(8,128)(2,1)}), bf16[256,128]{1,0:T(8,128)(2,1)}) %reduce-scatter.6.cloned.1.call-update) | async-done | bytes 65552 | tf_op jit(solution)/shard_map/reduce_scatter | solution.py:97
  283.1 3.2 fusion.6
  286.3 50.8 %all-gather.10.cloned.1.call-done = bf16[8192,128]{1,0:T(8,128)(2,1)} async-done(((bf16[256,128]{1,0:T(8,128)(2,1)}), bf16[8192,128]{1,0:T(8,128)(2,1)}) %all-gather.10.cloned.1.call-update) | async-done | bytes 2097168 | tf_op jit(solution)/shard_map/all_gather | solution.py:58
  337.1 5.7 multiply_reduce_fusion
  343.3 3.2 fusion.7
  346.5 7.8 %pad_maximum_fusion = bf16[4096,1024]{0,1:T(8,128)(2,1)} fusion(bf16[4096,512]{0,1:T(8,128)(2,1)} %fusion.7, bf16[4096,512]{0,1:T(8,128)(2,1)} %fusion.6), kind=kLoop, calls=%fused_computation.8 | loop fusion | flops 16777216 | bytes 16777216 | tf_op jit(solution)/shard_map/concatenate | solution.py:112
  354.3 12.0 %copy.47 = bf16[4096,1024]{1,0:T(8,128)(2,1)} copy(bf16[4096,1024]{0,1:T(8,128)(2,1)} %pad_maximum_fusion) | data formatting | bytes 16777216
  366.4 118.3 %reduce-scatter.10.cloned.1.call-done = bf16[128,1024]{1,0:T(8,128)(2,1)} async-done(((bf16[4096,1024]{1,0:T(8,128)(2,1)}), bf16[128,1024]{1,0:T(8,128)(2,1)}) %reduce-scatter.10.cloned.1.call-update) | async-done | bytes 262160
  486.8 4.8 fusion.2
  493.6 2.6 fusion.3
  496.2 5.0 fusion.9
  501.2 2.6 fusion.8
  506.8 25.7 %all-gather.16.cloned.1.call-done = bf16[1024,1024]{0,1:T(8,128)(2,1)} async-done(((bf16[128,1024]{0,1:T(8,128)(2,1)}), bf16[1024,1024]{0,1:T(8,128)(2,1)}) %all-gather.16.cloned.1.call-update) | async-done | bytes 2097168 | tf_op jit(solution)/shard_map/all_gather | solution.py:117
  532.5 2.4 copy.49
  538.1 91.2 %reduce-scatter.8.cloned.1.call-done = bf16[256,128]{1,0:T(8,128)(2,1)} async-done(((bf16[8192,128]{1,0:T(8,128)(2,1)}), bf16[256,128]{1,0:T(8,128)(2,1)}) %reduce-scatter.8.cloned.1.call-update) | async-done | bytes 65552 | tf_op jit(solution)/shard_map/reduce_scatter | solution.py:94
  (60 shorter events, 19.2 us)
Async XLA Ops:
  7.2 187.8 %copy-start = (bf16[1,256,4096]{2,1,0:T(8,128)(2,1)S(1)}, bf16[1,256,4096]{2,1,0:T(8,128)(2,1)}, u32[]{:S(2)}) copy-start(bf16[1,256,4096]{2,1,0:T(8,128)(2,1)} %param.11) | copy-start | bytes 6291460
  7.2 61.0 %all-gather.14.cloned.1.call-start = ((), (), s32[]{:S(2)}) async-start(), calls=%async_computation.8 | async-start | bytes 2162688 | tf_op jit(solution)/shard_map/all_gather | solution.py:57
  7.9 120.2 %all-gather.12.cloned.1.call-start = ((), (), s32[]{:S(2)}) async-start(), calls=%async_computation.5 | async-start | bytes 4325376 | tf_op jit(solution)/shard_map/all_gather | solution.py:50
  8.7 179.9 %all-gather.8.cloned.1.call-start = ((), (), s32[]{:S(2)}) async-start(), calls=%async_computation.3 | async-start | bytes 4325376 | tf_op jit(solution)/shard_map/all_gather | solution.py:49
  9.4 272.5 %reduce-scatter.6.cloned.1.call-start = ((), (), s32[]{:S(2)}) async-start(), calls=%async_computation.6 | async-start | bytes 2162688 | tf_op jit(solution)/shard_map/reduce_scatter | solution.py:97
  72.8 3.2 copy-start.2
  138.7 6.8 %copy-start.11 = (s32[1,256,2]{1,2,0:T(2,128)S(1)}, s32[1,256,2]{1,2,0:T(2,128)}, u32[]{:S(2)}) copy-start(s32[1,256,2]{1,2,0:T(2,128)} %param.16) | copy-start | bytes 6148
  138.7 6.8 %copy-start.10 = (f32[1,256,4]{1,2,0:T(4,128)S(1)}, f32[1,256,4]{1,2,0:T(4,128)}, u32[]{:S(2)}) copy-start(f32[1,256,4]{1,2,0:T(4,128)} %param.15) | copy-start | bytes 12292
  145.4 191.7 %all-gather.10.cloned.1.call-start = ((), (), s32[]{:S(2)}) async-start(), calls=%async_computation.4 | async-start | bytes 2162688 | tf_op jit(solution)/shard_map/all_gather | solution.py:58
  199.1 285.6 %reduce-scatter.10.cloned.1.call-start = ((), (), s32[]{:S(2)}) async-start(), calls=%async_computation.10 | async-start | bytes 8650752
  286.3 57.0 %copy-start.7 = (bf16[1,256,4096]{2,1,0:T(8,128)(2,1)S(1)}, bf16[1,256,4096]{2,1,0:T(8,128)(2,1)}, u32[]{:S(2)}) copy-start(bf16[1,256,4096]{2,1,0:T(8,128)(2,1)} %param.21) | copy-start | bytes 6291460
  366.3 120.5 %copy-start.6 = (bf16[8192,128]{1,0:T(8,128)(2,1)S(1)}, bf16[8192,128]{1,0:T(8,128)(2,1)}, u32[]{:S(2)}) copy-start(bf16[8192,128]{1,0:T(8,128)(2,1)} %all-gather.10.cloned.1.call-done) | copy-start | bytes 6291460
  366.4 166.2 %all-gather.16.cloned.1.call-start = ((), (), s32[]{:S(2)}) async-start(), calls=%async_computation.9 | async-start | bytes 2359296 | tf_op jit(solution)/shard_map/all_gather | solution.py:117
  486.5 142.8 %reduce-scatter.8.cloned.1.call-start = ((), (), s32[]{:S(2)}) async-start(), calls=%async_computation.7 | async-start | bytes 2162688 | tf_op jit(solution)/shard_map/reduce_scatter | solution.py:94
  486.8 6.8 %copy-start.9 = (bf16[1,256,128]{2,1,0:T(8,128)(2,1)S(1)}, bf16[1,256,128]{2,1,0:T(8,128)(2,1)}, u32[]{:S(2)}) copy-start(bf16[1,256,128]{2,1,0:T(8,128)(2,1)} %param.12) | copy-start | bytes 196612
  491.6 1.9 copy-start.3
  496.2 5.0 copy-start.5
  501.2 2.6 copy-start.4
  501.2 3.6 copy-start.8
  532.5 96.8 %copy-start.1 = (bf16[1,256,4096]{2,1,0:T(8,128)(2,1)S(1)}, bf16[1,256,4096]{2,1,0:T(8,128)(2,1)}, u32[]{:S(2)}) copy-start(bf16[1,256,4096]{2,1,0:T(8,128)(2,1)} %param.11) | copy-start | bytes 6291460
Sparse Core Ops, SparseCore 0:
  10.6 57.5 all-gather.13
  70.7 57.3 all-gather.11
  130.6 57.8 all-gather.7
  192.8 88.9 reduce-scatter.5
  284.8 52.2 all-gather.9
  366.5 118.1 reduce-scatter.9
  487.1 45.3 all-gather.15
  537.4 91.8 reduce-scatter.7
